TPU v7x, 32 devices: a whole 2x2x4 slice. The times are simulated.
32 devices in a mesh: row: 8 (over z, y), col: 4 (over x, core).
Axes of the slice: x: 2, y: 2, z: 4, core: 2. Of those that a mesh axis runs over, the one named last changes fastest.
Arguments:
- sub_field: float32 [65536, 128], P(('row', 'col')), may hold values from -2.4 to 2.4
- reluctivity: float32 [2, 65536, 128], P(None, ('row', 'col')), may hold values from 0.3 to 3
- stride: int32 [32], P(('row', 'col')), may hold values from 2 to 511
- counts: int32 [32, 8], P(('row', 'col')), may hold values from 1 to 32, as said below
- source_cell: int32 [32, 8, 32], P(('row', 'col')), may hold values from 0 to 2047
- target_row: int32 [8, 4, 8, 32], P('row', 'col'), may hold values from 0 to 2047
- lower_tiles: float32 [28, 2048, 2048], P(None, 'row', 'col'), may hold values from -0.046875 to 0.046875
- diag_inverse: float32 [8, 2048, 2048], P(None, 'col', 'row'), may hold values from -1 to 2, as said below
Outputs:
- solution: float32 [8, 4, 512, 128], P(None, 'col', 'row')
Inputs may be any that keep to these rules, and one draw needn't show every extreme that they name: `counts`: every subdomain sends at least one contribution to every grid row; in every draw one grid row receives 32 contributions from every subdomain. `diag_inverse`: block i is the given inverse of the window's diagonal block i.
All inputs are finite; a program needn't handle non-finite values.
Results may differ from a plain program's by a relative error of at most 0.0003.
Values sent between devices are 32-bit elements; how exact they have to be, the bound alone decides.
A program may use at most 128 MiB of HBM per device.

v0:
```python
import jax
import jax.numpy as jnp
from jax import lax
from jax.sharding import PartitionSpec as P


def exact_dot(left, right):
    return jnp.dot(left, right, precision=lax.Precision.HIGHEST, preferred_element_type=jnp.float32)


def sweep_subdomain(field, radial_nu, tangent_nu, stride_value):
    cell_index = jnp.arange(field.shape[0], dtype=jnp.int32)[:, None]
    radial_prev = jnp.where(cell_index >= stride_value, jnp.roll(field, stride_value, axis=0), 0.0)
    tangent_prev = jnp.where(cell_index >= 1, jnp.roll(field, 1, axis=0), 0.0)
    return radial_nu * (field - radial_prev) + tangent_nu * (field - tangent_prev)


def column_total(partial_rows):
    return lax.psum(partial_rows, "col")


def pair_index(later_block, earlier_block):
    return later_block * (later_block - 1) // 2 + earlier_block


def per_device(
    sub_field, reluctivity, stride, counts, source_cell, target_row, lower_tiles, diag_inverse
):
    blocks = diag_inverse.shape[0]
    tile_rows = lower_tiles.shape[1]
    share_rows = diag_inverse.shape[1]
    rotor = sub_field.shape[1]
    grid_rows = lax.axis_size("row")
    piece_rows = share_rows // grid_rows
    swept = sweep_subdomain(sub_field, reluctivity[0], reluctivity[1], stride[0])
    picked = swept[source_cell[0]]
    slots = source_cell.shape[2]
    live = jnp.arange(slots, dtype=jnp.int32)[None, :] < counts[0][:, None]
    picked = jnp.where(live[:, :, None], picked, 0.0)
    received = lax.all_to_all(picked, "row", split_axis=0, concat_axis=0, tiled=True)
    targets = target_row[0, 0].reshape(-1)
    interface = (
        jnp.zeros((blocks * tile_rows, rotor), jnp.float32)
        .at[targets]
        .add(received.reshape(-1, rotor))
    )
    interface = interface.reshape(blocks, tile_rows, rotor)
    pieces = []
    solved = []
    offset = lax.axis_index("row") * piece_rows
    for row_block in range(blocks):
        residual = interface[row_block]
        for earlier in range(row_block):
            residual = residual - exact_dot(
                lower_tiles[pair_index(row_block, earlier)], solved[earlier]
            )
        residual = column_total(residual)
        current = lax.psum(exact_dot(diag_inverse[row_block], residual), "row")
        solved.append(current)
        pieces.append(lax.dynamic_slice_in_dim(current, offset, piece_rows, 0))
    return jnp.stack(pieces)[:, None]


def solution(mesh):
    placed = (
        P(("row", "col"), None),
        P(None, ("row", "col"), None),
        P(("row", "col")),
        P(("row", "col"), None),
        P(("row", "col"), None, None),
        P("row", "col", None, None),
        P(None, "row", "col"),
        P(None, "col", "row"),
    )
    return jax.shard_map(
        per_device,
        mesh=mesh,
        in_specs=placed,
        out_specs=P(None, "col", "row", None),
        check_vma=False,
    )
```

profile of v0, /device:TPU:0, one launch (start us, length us, event | category | flops | bytes accessed | tf_op | source)
XLA Modules:
  0.0 899.2 jit_solution(8659680226856213526)
XLA Ops:
  9.4 4.2 fusion.32
  15.1 7.3 all-to-all-start
  23.2 6.5 all-to-all-done
  32.1 29.7 %all-reduce.17.cloned.1.call-done = f32[256,128]{1,0:T(8,128)} async-done(((f32[256,128]{1,0:T(8,128)}), f32[256,128]{1,0:T(8,128)}) %all-reduce.17.cloned.1.call-update) | async-done | bytes 131088 | tf_op jit(solution)/shard_map/psum | solution.py:19
  61.8 2.5 convolution_bitcast_fusion.7
  64.4 71.8 %all-reduce.19.cloned.1.call-done = f32[512,128]{0,1:T(8,128)} async-done(((f32[512,128]{0,1:T(8,128)}), f32[512,128]{0,1:T(8,128)}) %all-reduce.19.cloned.1.call-update) | async-done | bytes 262160 | tf_op jit(solution)/shard_map/psum | solution.py:58
  136.2 2.4 fusion.27
  138.7 1.7 fusion.6
  140.4 1.7 fusion.12
  142.1 1.7 fusion.17
  143.8 1.7 fusion.21
  145.5 1.7 fusion.24
  148.2 21.5 %all-reduce.21.cloned.1.call-done = f32[256,128]{1,0:T(8,128)} async-done(((f32[256,128]{1,0:T(8,128)}), f32[256,128]{1,0:T(8,128)}) %all-reduce.21.cloned.1.call-update) | async-done | bytes 131088 | tf_op jit(solution)/shard_map/psum | solution.py:19
  169.7 2.5 convolution_bitcast_fusion.6
  172.4 1.7 fusion.26
  174.1 69.9 %all-reduce.23.cloned.1.call-done = f32[512,128]{0,1:T(8,128)} async-done(((f32[512,128]{0,1:T(8,128)}), f32[512,128]{0,1:T(8,128)}) %all-reduce.23.cloned.1.call-update) | async-done | bytes 262160 | tf_op jit(solution)/shard_map/psum | solution.py:58
  244.0 2.4 fusion.25
  246.4 1.7 fusion.5
  249.9 1.7 fusion.16
  251.6 1.7 fusion.20
  254.3 23.2 %all-reduce.25.cloned.1.call-done = f32[256,128]{1,0:T(8,128)} async-done(((f32[256,128]{1,0:T(8,128)}), f32[256,128]{1,0:T(8,128)}) %all-reduce.25.cloned.1.call-update) | async-done | bytes 131088 | tf_op jit(solution)/shard_map/psum | solution.py:19
  277.5 2.5 convolution_bitcast_fusion.5
  282.1 69.8 %all-reduce.27.cloned.1.call-done = f32[512,128]{0,1:T(8,128)} async-done(((f32[512,128]{0,1:T(8,128)}), f32[512,128]{0,1:T(8,128)}) %all-reduce.27.cloned.1.call-update) | async-done | bytes 262160 | tf_op jit(solution)/shard_map/psum | solution.py:58
  351.8 2.4 fusion.22
  356.0 1.7 fusion.10
  357.7 1.7 fusion.15
  360.4 25.0 %all-reduce.29.cloned.1.call-done = f32[256,128]{1,0:T(8,128)} async-done(((f32[256,128]{1,0:T(8,128)}), f32[256,128]{1,0:T(8,128)}) %all-reduce.29.cloned.1.call-update) | async-done | bytes 131088 | tf_op jit(solution)/shard_map/psum | solution.py:19
  385.4 2.5 convolution_bitcast_fusion.4
  389.7 70.1 %all-reduce.31.cloned.1.call-done = f32[512,128]{0,1:T(8,128)} async-done(((f32[512,128]{0,1:T(8,128)}), f32[512,128]{0,1:T(8,128)}) %all-reduce.31.cloned.1.call-update) | async-done | bytes 262160 | tf_op jit(solution)/shard_map/psum | solution.py:58
  459.8 2.4 fusion.18
  466.6 26.6 %all-reduce.33.cloned.1.call-done = f32[256,128]{1,0:T(8,128)} async-done(((f32[256,128]{1,0:T(8,128)}), f32[256,128]{1,0:T(8,128)}) %all-reduce.33.cloned.1.call-update) | async-done | bytes 131088 | tf_op jit(solution)/shard_map/psum | solution.py:19
  493.3 2.5 convolution_bitcast_fusion.3
  497.6 69.9 %all-reduce.35.cloned.1.call-done = f32[512,128]{0,1:T(8,128)} async-done(((f32[512,128]{0,1:T(8,128)}), f32[512,128]{0,1:T(8,128)}) %all-reduce.35.cloned.1.call-update) | async-done | bytes 262160 | tf_op jit(solution)/shard_map/psum | solution.py:58
  567.5 2.4 fusion.13
  570.0 1.7 fusion.2
  571.7 29.4 %all-reduce.37.cloned.1.call-done = f32[256,128]{1,0:T(8,128)} async-done(((f32[256,128]{1,0:T(8,128)}), f32[256,128]{1,0:T(8,128)}) %all-reduce.37.cloned.1.call-update) | async-done | bytes 131088 | tf_op jit(solution)/shard_map/psum | solution.py:19
  601.1 2.5 convolution_bitcast_fusion.2
  604.7 1.7 fusion.8
  606.4 68.9 %all-reduce.39.cloned.1.call-done = f32[512,128]{0,1:T(8,128)} async-done(((f32[512,128]{0,1:T(8,128)}), f32[512,128]{0,1:T(8,128)}) %all-reduce.39.cloned.1.call-update) | async-done | bytes 262160 | tf_op jit(solution)/shard_map/psum | solution.py:58
  675.4 2.4 fusion.7
  677.8 31.1 %all-reduce.41.cloned.1.call-done = f32[256,128]{1,0:T(8,128)} async-done(((f32[256,128]{1,0:T(8,128)}), f32[256,128]{1,0:T(8,128)}) %all-reduce.41.cloned.1.call-update) | async-done | bytes 131088 | tf_op jit(solution)/shard_map/psum | solution.py:19
  708.9 2.5 convolution_bitcast_fusion.1
  712.5 1.7 fusion.1
  714.2 68.9 %all-reduce.43.cloned.1.call-done = f32[512,128]{0,1:T(8,128)} async-done(((f32[512,128]{0,1:T(8,128)}), f32[512,128]{0,1:T(8,128)}) %all-reduce.43.cloned.1.call-update) | async-done | bytes 262160 | tf_op jit(solution)/shard_map/psum | solution.py:58
  783.2 2.4 fusion
  785.6 31.1 %all-reduce.45.cloned.1.call-done = f32[256,128]{1,0:T(8,128)} async-done(((f32[256,128]{1,0:T(8,128)}), f32[256,128]{1,0:T(8,128)}) %all-reduce.45.cloned.1.call-update) | async-done | bytes 131088 | tf_op jit(solution)/shard_map/psum | solution.py:19
  816.7 2.5 convolution_bitcast_fusion
  820.3 70.7 %all-reduce.47.cloned.1.call-done = f32[512,128]{0,1:T(8,128)} async-done(((f32[512,128]{0,1:T(8,128)}), f32[512,128]{0,1:T(8,128)}) %all-reduce.47.cloned.1.call-update) | async-done | bytes 262160 | tf_op jit(solution)/shard_map/psum | solution.py:58
  (77 shorter events, 28.5 us)
Async XLA Ops:
  15.1 14.6 %all-to-all-start = ((f32[8,32,128]{2,1,0:T(8,128)}), f32[8,32,128]{2,1,0:T(8,128)S(1)}, u32[]{:S(2)}, u32[]{:S(2)}) async-start(f32[8,32,128]{2,1,0:T(8,128)} %broadcast_select_fusion), calls=%async_computation | async-start | bytes 262144 | tf_op jit(solution)/shard_map/all_to_all | solution.py:40
  22.4 39.4 %all-reduce.17.cloned.1.call-start = ((), (), s32[]{:S(2)}) async-start(), calls=%async_computation.1 | async-start | bytes 262144 | tf_op jit(solution)/shard_map/psum | solution.py:19
  32.1 104.1 %all-reduce.19.cloned.1.call-start = ((), (), s32[]{:S(2)}) async-start(), calls=%async_computation.2 | async-start | bytes 524288 | tf_op jit(solution)/shard_map/psum | solution.py:58
  64.4 105.4 %all-reduce.21.cloned.1.call-start = ((), (), s32[]{:S(2)}) async-start(), calls=%async_computation.3 | async-start | bytes 262144 | tf_op jit(solution)/shard_map/psum | solution.py:19
  138.6 105.4 %all-reduce.23.cloned.1.call-start = ((), (), s32[]{:S(2)}) async-start(), calls=%async_computation.4 | async-start | bytes 524288 | tf_op jit(solution)/shard_map/psum | solution.py:58
  172.3 105.2 %all-reduce.25.cloned.1.call-start = ((), (), s32[]{:S(2)}) async-start(), calls=%async_computation.5 | async-start | bytes 262144 | tf_op jit(solution)/shard_map/psum | solution.py:19
  246.4 105.4 %all-reduce.27.cloned.1.call-start = ((), (), s32[]{:S(2)}) async-start(), calls=%async_computation.6 | async-start | bytes 524288 | tf_op jit(solution)/shard_map/psum | solution.py:58
  280.1 105.2 %all-reduce.29.cloned.1.call-start = ((), (), s32[]{:S(2)}) async-start(), calls=%async_computation.7 | async-start | bytes 262144 | tf_op jit(solution)/shard_map/psum | solution.py:19
  354.2 105.6 %all-reduce.31.cloned.1.call-start = ((), (), s32[]{:S(2)}) async-start(), calls=%async_computation.8 | async-start | bytes 524288 | tf_op jit(solution)/shard_map/psum | solution.py:58
  387.9 105.4 %all-reduce.33.cloned.1.call-start = ((), (), s32[]{:S(2)}) async-start(), calls=%async_computation.9 | async-start | bytes 262144 | tf_op jit(solution)/shard_map/psum | solution.py:19
  462.2 105.4 %all-reduce.35.cloned.1.call-start = ((), (), s32[]{:S(2)}) async-start(), calls=%async_computation.10 | async-start | bytes 524288 | tf_op jit(solution)/shard_map/psum | solution.py:58
  495.8 105.2 %all-reduce.37.cloned.1.call-start = ((), (), s32[]{:S(2)}) async-start(), calls=%async_computation.11 | async-start | bytes 262144 | tf_op jit(solution)/shard_map/psum | solution.py:19
  569.9 105.4 %all-reduce.39.cloned.1.call-start = ((), (), s32[]{:S(2)}) async-start(), calls=%async_computation.12 | async-start | bytes 524288 | tf_op jit(solution)/shard_map/psum | solution.py:58
  603.6 105.2 %all-reduce.41.cloned.1.call-start = ((), (), s32[]{:S(2)}) async-start(), calls=%async_computation.13 | async-start | bytes 262144 | tf_op jit(solution)/shard_map/psum | solution.py:19
  677.8 105.4 %all-reduce.43.cloned.1.call-start = ((), (), s32[]{:S(2)}) async-start(), calls=%async_computation.14 | async-start | bytes 524288 | tf_op jit(solution)/shard_map/psum | solution.py:58
  711.5 105.2 %all-reduce.45.cloned.1.call-start = ((), (), s32[]{:S(2)}) async-start(), calls=%async_computation.15 | async-start | bytes 262144 | tf_op jit(solution)/shard_map/psum | solution.py:19
  785.6 105.4 %all-reduce.47.cloned.1.call-start = ((), (), s32[]{:S(2)}) async-start(), calls=%async_computation.16 | async-start | bytes 524288 | tf_op jit(solution)/shard_map/psum | solution.py:58
  892.0 0.7 copy-start
Sparse Core Ops, SparseCore 0:
  32.2 29.5 all-reduce.16
  65.2 71.0 all-reduce.18
  138.7 30.9 all-reduce.20
  172.9 71.0 all-reduce.22
  246.5 30.9 all-reduce.24
  280.7 71.0 all-reduce.26
  354.3 30.9 all-reduce.28
  388.7 71.0 all-reduce.30
  462.3 30.9 all-reduce.32
  496.5 71.0 all-reduce.34
  570.1 30.9 all-reduce.36
  604.3 71.0 all-reduce.38
  677.9 30.9 all-reduce.40
  712.1 71.0 all-reduce.42
  785.7 30.9 all-reduce.44
  819.9 71.0 all-reduce.46
where the time goes:
time: 901 us; the launch traced here: 899 us
  waiting for transfers between devices  784 us (87%)
  matrix products  72.7 us (8%)
  between operations  14.3 us (2%)
  local copies, waits for them, and re-layouts  11.6 us (1%)
    psum x8, waiting for transfers between devices, per_device(): current = lax.psum(exact_dot(diag_inverse[row_block], residual), 'row')  560 us
    psum x8, waiting for transfers between devices, column_total(): return lax.psum(partial_rows, 'col')  218 us
    dot_general x36, matrix products, exact_dot(): jnp.dot(left, right, precision=lax.Precision.HIGHEST, preferred_element_t...  72.7 us
  transfers between devices with their start and end apart: 17, of which 17 were waited for; matrix products, arithmetic and copies ran while one was open for 5% of the time, Pallas kernels for 0%

commit v1 on v0

v1 whole, which is shorter than its diff:
```python
import functools

import jax
import jax.numpy as jnp
from jax import lax
from jax.experimental import pallas as pl
from jax.experimental.pallas import tpu as pltpu
from jax.sharding import PartitionSpec as P

MESH = pl.DeviceIdType.MESH
QUAD = 4
CORES = 2


def sweep_subdomain(field, radial_nu, tangent_nu, stride_value):
    cell_index = jnp.arange(field.shape[0], dtype=jnp.int32)[:, None]
    radial_prev = jnp.where(cell_index >= stride_value, jnp.roll(field, stride_value, axis=0), 0.0)
    tangent_prev = jnp.where(cell_index >= 1, jnp.roll(field, 1, axis=0), 0.0)
    return radial_nu * (field - radial_prev) + tangent_nu * (field - tangent_prev)


def pair_index(later_block, earlier_block):
    return later_block * (later_block - 1) // 2 + earlier_block


def halves(value, axis):
    high = value.astype(jnp.bfloat16)
    low = (value - high.astype(jnp.float32)).astype(jnp.bfloat16)
    return jnp.concatenate([high, low], axis=axis)


def split_product(left, right_halves):
    rows, rotor = left.shape[0], right_halves.shape[1] // 2
    full = jnp.dot(halves(left, 0), right_halves, preferred_element_type=jnp.float32)
    return (full[rows:, rotor:] + full[rows:, :rotor] + full[:rows, rotor:]) + full[:rows, :rotor]


def solve_kernel(
    n_row, n_col, rhs_ref, lower_hbm, diag_hbm, out_ref,
    lower, diag, acc, c1_in, c2_src, c2_in, res, part, a_in, b_src, b_in, ysh, yb,
    w_sem, d_sem, send_sem, recv_sem, c2_send, c2_recv,
):
    blocks = diag.shape[0]
    pairs = lower.shape[0]
    n_quads = n_row // QUAD
    n_x = n_col // CORES
    r = lax.axis_index("row")
    c = lax.axis_index("col")
    a, b = lax.rem(r, QUAD), lax.div(r, QUAD)
    core = lax.rem(c, CORES)
    core_peer = c + 1 - 2 * core
    x_peer = [lax.rem(c + CORES * s, n_col) for s in range(1, n_x)]
    a_off = [lax.rem(a + s, QUAD) for s in range(1, QUAD)]
    a_peer = [b * QUAD + o for o in a_off]
    b_off = [lax.rem(b + s, n_quads) for s in range(1, n_quads)]
    b_peer = [o * QUAD + a for o in b_off]

    def load_lower(k):
        return pltpu.make_async_copy(lower_hbm.at[k], lower.at[k], w_sem.at[k])

    def load_diag(k):
        return pltpu.make_async_copy(diag_hbm.at[k], diag.at[k], d_sem.at[k])

    for i in range(blocks):
        load_diag(i).start()
        for j in range(i):
            load_lower(pair_index(i, j)).start()

    barrier = pltpu.get_barrier_semaphore()
    pl.semaphore_signal(barrier, inc=1, device_id={"col": core_peer}, device_id_type=MESH)
    for p in x_peer:
        pl.semaphore_signal(barrier, inc=1, device_id={"col": p}, device_id_type=MESH)
    for p in a_peer + b_peer:
        pl.semaphore_signal(barrier, inc=1, device_id={"row": p}, device_id_type=MESH)
    acc[...] = rhs_ref[...]
    pl.semaphore_wait(barrier, 1 + len(x_peer) + len(a_peer) + len(b_peer))

    def remote(src, dst, k, device):
        return pltpu.make_async_remote_copy(
            src_ref=src, dst_ref=dst, send_sem=send_sem.at[k], recv_sem=recv_sem.at[k],
            device_id=device, device_id_type=MESH,
        )

    k_a = 2
    k_b = k_a + QUAD - 1
    k_bg = k_b + max(n_quads - 1, 0)
    k_ag = k_bg + max(n_quads - 1, 0)

    half_rows = acc.shape[2]
    rotor = acc.shape[3]

    def lower_step(i, j):
        k = pair_index(i, j)
        load_lower(k).wait()
        product = split_product(lower[k], yb[...])
        acc[i] = acc[i] - product.reshape(CORES, half_rows, rotor)

    def run(copies, work=None):
        for copy in copies:
            copy.start()
        if work is not None:
            work()
        for copy in copies:
            copy.wait()

    def step(i, carry):
        def deferred(*slots):
            def work():
                for t in slots:
                    @pl.when(jnp.logical_and(i > 0, i + 1 + t < blocks))
                    def _():
                        lower_step(i + 1 + t, i - 1)
            return work

        @pl.when(i > 0)
        def _():
            lower_step(i, i - 1)

        run([remote(acc.at[i, 1 - core], c1_in, 0, {"col": core_peer})])
        c2_src[...] = acc[i, core] + c1_in[...]
        parity = lax.rem(i, 2)
        run(
            [
                pltpu.make_async_remote_copy(
                    src_ref=c2_src, dst_ref=c2_in.at[parity, s], send_sem=c2_send.at[parity, s],
                    recv_sem=c2_recv.at[parity, s], device_id={"col": p}, device_id_type=MESH,
                )
                for s, p in enumerate(x_peer)
            ],
            deferred(0),
        )
        total = c2_src[...]
        for s in range(n_x - 1):
            total = total + c2_in[parity, s]
        res[core] = total
        load_diag(i).wait()
        run([remote(res.at[core], res.at[core], 1, {"col": core_peer})])

        residual = res[...].reshape(CORES * half_rows, rotor)
        part[...] = split_product(diag[i], halves(residual, 1)).reshape(part.shape)
        run(
            [
                remote(part.at[:, o], a_in.at[s], k_a + s, {"row": p})
                for s, (o, p) in enumerate(zip(a_off, a_peer))
            ],
            deferred(1, 2),
        )
        total = part[:, a]
        for s in range(QUAD - 1):
            total = total + a_in[s]
        b_src[...] = total
        run(
            [
                remote(b_src.at[o], b_in.at[s], k_b + s, {"row": p})
                for s, (o, p) in enumerate(zip(b_off, b_peer))
            ],
            deferred(3),
        )
        total = b_src[b]
        for s in range(n_quads - 1):
            total = total + b_in[s]
        ysh[b, a] = total
        out_ref[i] = total

        @pl.when(i < blocks - 1)
        def _():
            run(
                [
                    remote(ysh.at[b, a], ysh.at[b, a], k_bg + s, {"row": p})
                    for s, p in enumerate(b_peer)
                ],
                deferred(4),
            )
            run(
                [
                    remote(ysh.at[:, a], ysh.at[:, a], k_ag + s, {"row": p})
                    for s, p in enumerate(a_peer)
                ],
                deferred(5),
            )
            yb[...] = halves(ysh[...].reshape(yb.shape[0], rotor), 1)

        return carry

    lax.fori_loop(0, blocks, step, 0)


def solve(interface, lower_tiles, diag_inverse):
    n_row, n_col = lax.axis_size("row"), lax.axis_size("col")
    blocks, tile_rows, rotor = interface.shape
    pairs = lower_tiles.shape[0]
    share = diag_inverse.shape[1]
    piece = share // n_row
    quads = n_row // QUAD
    n_x = n_col // CORES
    half = tile_rows // CORES
    f32 = jnp.float32
    copies = 2 + 2 * (QUAD - 1) + 2 * (quads - 1)
    vmem = pl.BlockSpec(memory_space=pltpu.VMEM)
    hbm = pl.BlockSpec(memory_space=pl.ANY)
    return pl.pallas_call(
        functools.partial(solve_kernel, n_row, n_col),
        out_shape=jax.ShapeDtypeStruct((blocks, piece, rotor), f32),
        in_specs=[vmem, hbm, hbm],
        out_specs=vmem,
        scratch_shapes=[
            pltpu.VMEM(lower_tiles.shape, f32),
            pltpu.VMEM(diag_inverse.shape, f32),
            pltpu.VMEM((blocks, CORES, half, rotor), f32),
            pltpu.VMEM((half, rotor), f32),
            pltpu.VMEM((half, rotor), f32),
            pltpu.VMEM((2, n_x - 1, half, rotor), f32),
            pltpu.VMEM((CORES, half, rotor), f32),
            pltpu.VMEM((quads, QUAD, piece, rotor), f32),
            pltpu.VMEM((QUAD - 1, quads, piece, rotor), f32),
            pltpu.VMEM((quads, piece, rotor), f32),
            pltpu.VMEM((quads - 1, piece, rotor), f32),
            pltpu.VMEM((quads, QUAD, piece, rotor), f32),
            pltpu.VMEM((share, 2 * rotor), jnp.bfloat16),
            pltpu.SemaphoreType.DMA((pairs,)),
            pltpu.SemaphoreType.DMA((blocks,)),
            pltpu.SemaphoreType.DMA((copies,)),
            pltpu.SemaphoreType.DMA((copies,)),
            pltpu.SemaphoreType.DMA((2, n_x - 1)),
            pltpu.SemaphoreType.DMA((2, n_x - 1)),
        ],
        compiler_params=pltpu.CompilerParams(
            collective_id=0, has_side_effects=True, vmem_limit_bytes=48 * 1024 * 1024
        ),
    )(interface.reshape(blocks, CORES, half, rotor), lower_tiles, diag_inverse)


def per_device(
    sub_field, reluctivity, stride, counts, source_cell, target_row, lower_tiles, diag_inverse
):
    blocks = diag_inverse.shape[0]
    tile_rows = lower_tiles.shape[1]
    rotor = sub_field.shape[1]
    swept = sweep_subdomain(sub_field, reluctivity[0], reluctivity[1], stride[0])
    picked = swept[source_cell[0]]
    slots = source_cell.shape[2]
    live = jnp.arange(slots, dtype=jnp.int32)[None, :] < counts[0][:, None]
    picked = jnp.where(live[:, :, None], picked, 0.0)
    received = lax.all_to_all(picked, "row", split_axis=0, concat_axis=0, tiled=True)
    targets = target_row[0, 0].reshape(-1)
    interface = (
        jnp.zeros((blocks * tile_rows, rotor), jnp.float32)
        .at[targets]
        .add(received.reshape(-1, rotor))
    )
    interface = interface.reshape(blocks, tile_rows, rotor)
    return solve(interface, lower_tiles, diag_inverse)[:, None]


def solution(mesh):
    placed = (
        P(("row", "col"), None),
        P(None, ("row", "col"), None),
        P(("row", "col")),
        P(("row", "col"), None),
        P(("row", "col"), None, None),
        P("row", "col", None, None),
        P(None, "row", "col"),
        P(None, "col", "row"),
    )
    return jax.shard_map(
        per_device,
        mesh=mesh,
        in_specs=placed,
        out_specs=P(None, "col", "row", None),
        check_vma=False,
    )
```

time: 901 us -> 203 us (0.23)
  waiting for transfers between devices: 784 us -> 7.25 us
  Pallas kernels: 0 us -> 175 us
  matrix products: 72.7 us -> 0 us
  between operations: 14.3 us -> 0.71 us
    psum x16 -> x0, waiting for transfers between devices: 778 us -> none  [the longest x8 560 us: per_device(): current = lax.psum(exact_dot(diag_inverse[row_block], residual), 'row')]
    pallas_call x0 -> x1, Pallas kernels: none -> 175 us  [solve(): pl.pallas_call(functools.partial(solve_kernel, n_row, n_col), out_shape=j...]
    dot_general x36 -> x0, matrix products: 72.7 us -> none  [exact_dot(): jnp.dot(left, right, precision=lax.Precision.HIGHEST, preferred_element_t...]
  transfers between devices with their start and end apart: 17 -> 1, of which waited for: 17 -> 1; matrix products, arithmetic and copies ran while one was open for 5% -> 0% of each run, Pallas kernels for 0% -> 0%
where the time goes in v1:
time: 203 us
  Pallas kernels  175 us (86%)
  other arithmetic  8.02 us (4%)
  starting transfers between devices  7.3 us (4%)
  waiting for transfers between devices  7.25 us (4%)
  local copies, waits for them, and re-layouts  4.47 us (2%)
    pallas_call x1, Pallas kernels, solve(): pl.pallas_call(functools.partial(solve_kernel, n_row, n_col), out_shape=j...  175 us
    all_to_all x1, starting transfers between devices, per_device(): lax.all_to_all(picked, 'row', split_axis=0, concat_axis=0, tiled=True)  7.3 us
    all_to_all x1, waiting for transfers between devices, per_device(): lax.all_to_all(picked, 'row', split_axis=0, concat_axis=0, tiled=True)  7.25 us
    add x1, other arithmetic, sweep_subdomain(): radial_nu * (field - radial_prev) + tangent_nu * (field - tangent_prev)  4.15 us
  transfers between devices with their start and end apart: 1, of which 1 were waited for; matrix products, arithmetic and copies ran while one was open for 0% of the time, Pallas kernels for 0%

profile of v1, /device:TPU:0, one launch (start us, length us, event | category | flops | bytes accessed | tf_op | source)
XLA Modules:
  0.0 202.7 jit_solution(8231707591400841543)
XLA Ops:
  0.7 0.7 slice.16
  1.4 0.7 iota_compare_fusion.2
  2.1 0.7 compare_select_fusion
  2.8 0.1 reshape.96
  2.9 0.0 copy-start.1
  2.9 4.2 %fusion.4 = f32[2048,128]{1,0:T(8,128)S(1)} fusion(f32[2048,128]{1,0:T(8,128)} %param.8, s32[]{:T(128)S(6)} %select_n.46, f32[2047,128]{1,0:T(8,128)} %bitcast.26, f32[1,128]{1,0:T(1,128)S(1)} %slice.16, f32[2,2048,128]{2,1,0:T(8,128)} %param.9, pred[2048]{0:T(1024)(128)(4,1)S(1)} %get-tuple-element.5, pred[2048]{0:T(1024)(128)(4,1)S(1)} %get-tuple-element.6), kind=kLoop, calls=%fused_computation.8 | loop fusion | flops 2359296 | bytes 5246980 | tf_op jit(solution)/shard_map/add | solution.py:19
  7.0 0.7 gather_fusion
  7.8 0.8 broadcast_select_fusion
  8.5 7.3 %all-to-all-start = ((f32[8,32,128]{2,1,0:T(8,128)}), f32[8,32,128]{2,1,0:T(8,128)S(1)}, u32[]{:S(2)}, u32[]{:S(2)}) async-start(f32[8,32,128]{2,1,0:T(8,128)} %broadcast_select_fusion), calls=%async_computation | async-start | bytes 262144 | tf_op jit(solution)/shard_map/all_to_all | solution.py:244
  15.8 0.0 copy-done.1
  15.8 0.1 reshape_squeeze.3
  15.9 7.3 %all-to-all-done = f32[8,32,128]{2,1,0:T(8,128)S(1)} async-done(((f32[8,32,128]{2,1,0:T(8,128)}), f32[8,32,128]{2,1,0:T(8,128)S(1)}, u32[]{:S(2)}, u32[]{:S(2)}) %all-to-all-start) | async-done | bytes 131104 | tf_op jit(solution)/shard_map/all_to_all | solution.py:244
  23.2 1.7 scatter_custom_fusion
  24.9 0.0 copy-start
  24.9 2.2 %copy-done = f32[8,512,256]{2,1,0:T(8,128)S(1)} copy-done((f32[8,512,256]{2,1,0:T(8,128)S(1)}, f32[8,512,256]{2,1,0:T(8,128)}, u32[]{:S(2)}) %copy-start) | copy-done | bytes 4194328
  27.0 174.9 %shard_map.82 = f32[8,64,128]{2,1,0:T(8,128)S(1)} custom-call(f32[8,2,128,128]{3,2,1,0:T(8,128)S(1)} %bitcast.24, f32[28,256,512]{2,1,0:T(8,128)} %lower_hbm.1, f32[8,512,256]{2,1,0:T(8,128)S(1)} %copy-done), custom_call_target="tpu_custom_call" | custom-call | tf_op jit(solution)/shard_map/pallas_call | solution.py:201
  202.0 0.7 copy.12
  (3 shorter events, 0.0 us)
Async XLA Ops:
  2.9 12.9 %copy-start.1 = (s32[1,1,8,32]{3,2,1,0:T(8,128)S(1)}, s32[1,1,8,32]{3,2,1,0:T(8,128)}, u32[]{:S(2)}) copy-start(s32[1,1,8,32]{3,2,1,0:T(8,128)} %param.13) | copy-start | bytes 3076
  8.5 14.6 %all-to-all-start = ((f32[8,32,128]{2,1,0:T(8,128)}), f32[8,32,128]{2,1,0:T(8,128)S(1)}, u32[]{:S(2)}, u32[]{:S(2)}) async-start(f32[8,32,128]{2,1,0:T(8,128)} %broadcast_select_fusion), calls=%async_computation | async-start | bytes 262144 | tf_op jit(solution)/shard_map/all_to_all | solution.py:244
  24.9 2.2 %copy-start = (f32[8,512,256]{2,1,0:T(8,128)S(1)}, f32[8,512,256]{2,1,0:T(8,128)}, u32[]{:S(2)}) copy-start(f32[8,512,256]{2,1,0:T(8,128)} %diag_hbm.1) | copy-start | bytes 12582916

commit v2 on v1

v2 whole, which is shorter than its diff:
```python
import functools

import jax
import jax.numpy as jnp
from jax import lax
from jax.experimental import pallas as pl
from jax.experimental.pallas import tpu as pltpu
from jax.sharding import PartitionSpec as P

MESH = pl.DeviceIdType.MESH
QUAD = 4
CORES = 2


def sweep_subdomain(field, radial_nu, tangent_nu, stride_value):
    cell_index = jnp.arange(field.shape[0], dtype=jnp.int32)[:, None]
    radial_prev = jnp.where(cell_index >= stride_value, jnp.roll(field, stride_value, axis=0), 0.0)
    tangent_prev = jnp.where(cell_index >= 1, jnp.roll(field, 1, axis=0), 0.0)
    return radial_nu * (field - radial_prev) + tangent_nu * (field - tangent_prev)


def pair_index(later_block, earlier_block):
    return later_block * (later_block - 1) // 2 + earlier_block


def halves(value, axis):
    high = value.astype(jnp.bfloat16)
    low = (value - high.astype(jnp.float32)).astype(jnp.bfloat16)
    return jnp.concatenate([high, low], axis=axis)


def split_product(left, right_halves):
    rows, rotor = left.shape[0], right_halves.shape[1] // 2
    full = jnp.dot(halves(left, 0), right_halves, preferred_element_type=jnp.float32)
    return (full[rows:, rotor:] + full[rows:, :rotor] + full[:rows, rotor:]) + full[:rows, :rotor]


def solve_kernel(
    n_row, n_col, rhs_ref, lower_hbm, diag_hbm, out_ref,
    lower, diag, acc, c1_in, c2_src, c2_in, res, part, a_in, b_src, b_in, ysh, yb,
    w_sem, d_sem, c1_sems, c2_sems, c3_sems, a_sems, b_sems, g_sems,
):
    blocks = diag.shape[0]
    n_quads = n_row // QUAD
    n_x = n_col // CORES
    chunks, chunk_rows, rotor = acc.shape[2:]
    half_rows = chunks * chunk_rows
    chunk_share = diag.shape[1] // n_quads
    r = lax.axis_index("row")
    c = lax.axis_index("col")
    a, b = lax.rem(r, QUAD), lax.div(r, QUAD)
    core = lax.rem(c, CORES)
    other = 1 - core
    core_peer = {"col": c + 1 - 2 * core}
    x_peer = [{"col": lax.rem(c + CORES * s, n_col)} for s in range(1, n_x)]
    a_off = [lax.rem(a + s, QUAD) for s in range(1, QUAD)]
    a_peer = [{"row": b * QUAD + o} for o in a_off]
    b_peer = [{"row": lax.rem(b + s, n_quads) * QUAD + a} for s in range(1, n_quads)]
    peers = [core_peer] + x_peer + a_peer + b_peer

    def load_lower(k):
        return pltpu.make_async_copy(lower_hbm.at[k], lower.at[k], w_sem.at[k])

    def load_diag(k):
        return pltpu.make_async_copy(diag_hbm.at[k], diag.at[k], d_sem.at[k])

    for i in range(blocks):
        load_diag(i).start()
        for j in range(i):
            load_lower(pair_index(i, j)).start()

    barrier = pltpu.get_barrier_semaphore()
    for p in peers:
        pl.semaphore_signal(barrier, inc=1, device_id=p, device_id_type=MESH)
    acc[...] = rhs_ref[...]
    pl.semaphore_wait(barrier, len(peers))

    def remote(src, dst, sems, at, device):
        copy = pltpu.make_async_remote_copy(
            src_ref=src, dst_ref=dst, send_sem=sems.at[(0,) + at], recv_sem=sems.at[(1,) + at],
            device_id=device, device_id_type=MESH,
        )
        copy.start()
        return copy

    def finish(copies):
        for copy in copies:
            copy.wait()

    def lower_step(i, j):
        k = pair_index(i, j)
        load_lower(k).wait()
        product = split_product(lower[k], yb[...])
        acc[i] = acc[i] - product.reshape(acc.shape[1:])

    def lower_half(i, side):
        start = pl.multiple_of(side * half_rows, half_rows)
        product = split_product(lower[pair_index(i, i - 1), pl.ds(start, half_rows)], yb[...])
        acc[i, side] = acc[i, side] - product.reshape(acc.shape[2:])

    def step(i, carry):
        parity = lax.rem(i, 2)

        def deferred(*slots):
            for t in slots:
                @pl.when(jnp.logical_and(i > 0, i + 1 + t < blocks))
                def _():
                    lower_step(i + 1 + t, i - 1)

        @pl.when(i > 0)
        def _():
            load_lower(pair_index(i, i - 1)).wait()
            lower_half(i, other)

        c1 = [
            remote(acc.at[i, other, q], c1_in.at[q], c1_sems, (q,), core_peer)
            for q in range(chunks)
        ]

        @pl.when(i > 0)
        def _():
            lower_half(i, core)

        c2 = []
        for q in range(chunks):
            c1[q].wait()
            c2_src[q] = acc[i, core, q] + c1_in[q]
            c2.append([
                remote(c2_src.at[q], c2_in.at[parity, q, s], c2_sems, (parity, q, s), p)
                for s, p in enumerate(x_peer)
            ])
        deferred(0)
        c3 = []
        for q in range(chunks):
            finish(c2[q])
            total = c2_src[q]
            for s in range(n_x - 1):
                total = total + c2_in[parity, q, s]
            res[core, q] = total
            c3.append(remote(res.at[core, q], res.at[core, q], c3_sems, (q,), core_peer))
        load_diag(i).wait()
        finish(c3)

        residual = halves(res[...].reshape(CORES * half_rows, rotor), 1)
        a_copies = []
        for h in range(n_quads):
            rows = diag[i, h * chunk_share:(h + 1) * chunk_share]
            part[h] = split_product(rows, residual).reshape(part.shape[1:])
            a_copies.append([
                remote(part.at[h, o], a_in.at[h, s], a_sems, (h, s), p)
                for s, (o, p) in enumerate(zip(a_off, a_peer))
            ])
        deferred(1, 2)
        b_copies = []
        for h in range(n_quads):
            finish(a_copies[h])
            total = part[h, a]
            for s in range(QUAD - 1):
                total = total + a_in[h, s]
            b_src[h] = total
            b_copies.append([
                remote(b_src.at[h], b_in.at[parity, h, s], b_sems, (parity, h, s), p)
                for s, p in enumerate(b_peer)
            ])
        deferred(3)

        def across(h):
            finish(b_copies[h])
            total = b_src[h]
            for s in range(n_quads - 1):
                total = total + b_in[parity, h, s]
            ysh[h, a] = total

        @pl.when(i < blocks - 1)
        def _():
            back = []
            for h in range(n_quads):
                across(h)
                back.append([
                    remote(ysh.at[h, a], ysh.at[h, a], g_sems, (h, s), p)
                    for s, p in enumerate(a_peer)
                ])
            deferred(4, 5)
            for h in range(n_quads):
                finish(back[h])
            yb[...] = halves(ysh[...].reshape(yb.shape[0], rotor), 1)

        @pl.when(i == blocks - 1)
        def _():
            for h in range(n_quads):
                across(h)

        out_ref[i] = ysh[b, a]
        return carry

    lax.fori_loop(0, blocks, step, 0)


def solve(interface, lower_tiles, diag_inverse):
    n_row, n_col = lax.axis_size("row"), lax.axis_size("col")
    blocks, tile_rows, rotor = interface.shape
    pairs = lower_tiles.shape[0]
    share = diag_inverse.shape[1]
    piece = share // n_row
    quads = n_row // QUAD
    n_x = n_col // CORES
    chunks = 2
    col_chunk = (chunks, tile_rows // CORES // chunks, rotor)
    f32 = jnp.float32
    vmem = pl.BlockSpec(memory_space=pltpu.VMEM)
    hbm = pl.BlockSpec(memory_space=pl.ANY)
    dma = pltpu.SemaphoreType.DMA
    return pl.pallas_call(
        functools.partial(solve_kernel, n_row, n_col),
        out_shape=jax.ShapeDtypeStruct((blocks, piece, rotor), f32),
        in_specs=[vmem, hbm, hbm],
        out_specs=vmem,
        scratch_shapes=[
            pltpu.VMEM(lower_tiles.shape, f32),
            pltpu.VMEM(diag_inverse.shape, f32),
            pltpu.VMEM((blocks, CORES) + col_chunk, f32),
            pltpu.VMEM(col_chunk, f32),
            pltpu.VMEM(col_chunk, f32),
            pltpu.VMEM((2, chunks, n_x - 1) + col_chunk[1:], f32),
            pltpu.VMEM((CORES,) + col_chunk, f32),
            pltpu.VMEM((quads, QUAD, piece, rotor), f32),
            pltpu.VMEM((quads, QUAD - 1, piece, rotor), f32),
            pltpu.VMEM((quads, piece, rotor), f32),
            pltpu.VMEM((2, quads, quads - 1, piece, rotor), f32),
            pltpu.VMEM((quads, QUAD, piece, rotor), f32),
            pltpu.VMEM((share, 2 * rotor), jnp.bfloat16),
            dma((pairs,)),
            dma((blocks,)),
            dma((2, chunks)),
            dma((2, 2, chunks, n_x - 1)),
            dma((2, chunks)),
            dma((2, quads, QUAD - 1)),
            dma((2, 2, quads, quads - 1)),
            dma((2, quads, QUAD - 1)),
        ],
        compiler_params=pltpu.CompilerParams(
            collective_id=0, has_side_effects=True, vmem_limit_bytes=48 * 1024 * 1024
        ),
    )(interface.reshape((blocks, CORES) + col_chunk), lower_tiles, diag_inverse)


def per_device(
    sub_field, reluctivity, stride, counts, source_cell, target_row, lower_tiles, diag_inverse
):
    blocks = diag_inverse.shape[0]
    tile_rows = lower_tiles.shape[1]
    rotor = sub_field.shape[1]
    swept = sweep_subdomain(sub_field, reluctivity[0], reluctivity[1], stride[0])
    picked = swept[source_cell[0]]
    slots = source_cell.shape[2]
    live = jnp.arange(slots, dtype=jnp.int32)[None, :] < counts[0][:, None]
    picked = jnp.where(live[:, :, None], picked, 0.0)
    received = lax.all_to_all(picked, "row", split_axis=0, concat_axis=0, tiled=True)
    targets = target_row[0, 0].reshape(-1)
    interface = (
        jnp.zeros((blocks * tile_rows, rotor), jnp.float32)
        .at[targets]
        .add(received.reshape(-1, rotor))
    )
    interface = interface.reshape(blocks, tile_rows, rotor)
    return solve(interface, lower_tiles, diag_inverse)[:, None]


def solution(mesh):
    placed = (
        P(("row", "col"), None),
        P(None, ("row", "col"), None),
        P(("row", "col")),
        P(("row", "col"), None),
        P(("row", "col"), None, None),
        P("row", "col", None, None),
        P(None, "row", "col"),
        P(None, "col", "row"),
    )
    return jax.shard_map(
        per_device,
        mesh=mesh,
        in_specs=placed,
        out_specs=P(None, "col", "row", None),
        check_vma=False,
    )
```

time: 203 us -> 178 us (0.88)
  Pallas kernels: 175 us -> 150 us
    pallas_call x1, Pallas kernels: 175 us -> 150 us  [solve(): pl.pallas_call(functools.partial(solve_kernel, n_row, n_col), out_shape=j...]
where the time goes in v2:
time: 178 us
  Pallas kernels  150 us (84%)
  other arithmetic  8.04 us (5%)
  starting transfers between devices  7.31 us (4%)
  waiting for transfers between devices  7.25 us (4%)
  local copies, waits for them, and re-layouts  4.47 us (3%)
    pallas_call x1, Pallas kernels, solve(): pl.pallas_call(functools.partial(solve_kernel, n_row, n_col), out_shape=j...  150 us
    all_to_all x1, starting transfers between devices, per_device(): lax.all_to_all(picked, 'row', split_axis=0, concat_axis=0, tiled=True)  7.31 us
    all_to_all x1, waiting for transfers between devices, per_device(): lax.all_to_all(picked, 'row', split_axis=0, concat_axis=0, tiled=True)  7.25 us
    add x1, other arithmetic, sweep_subdomain(): radial_nu * (field - radial_prev) + tangent_nu * (field - tangent_prev)  4.17 us
  transfers between devices with their start and end apart: 1, of which 1 were waited for; matrix products, arithmetic and copies ran while one was open for 0% of the time, Pallas kernels for 0%

profile of v2, /device:TPU:0, one launch (start us, length us, event | category | flops | bytes accessed | tf_op | source)
XLA Modules:
  0.0 177.7 jit_solution(14955764066233894399)
XLA Ops:
  0.7 0.7 slice.16
  1.4 0.7 iota_compare_fusion.2
  2.1 0.7 compare_select_fusion
  2.8 0.1 reshape.96
  2.9 0.0 copy-start.1
  2.9 4.2 %fusion.4 = f32[2048,128]{1,0:T(8,128)S(1)} fusion(f32[2048,128]{1,0:T(8,128)} %param.8, s32[]{:T(128)S(6)} %select_n.46, f32[2047,128]{1,0:T(8,128)} %bitcast.26, f32[1,128]{1,0:T(1,128)S(1)} %slice.16, f32[2,2048,128]{2,1,0:T(8,128)} %param.9, pred[2048]{0:T(1024)(128)(4,1)S(1)} %get-tuple-element.5, pred[2048]{0:T(1024)(128)(4,1)S(1)} %get-tuple-element.6), kind=kLoop, calls=%fused_computation.8 | loop fusion | flops 2359296 | bytes 5246980 | tf_op jit(solution)/shard_map/add | solution.py:19
  7.1 0.7 gather_fusion
  7.8 0.8 broadcast_select_fusion
  8.5 7.3 %all-to-all-start = ((f32[8,32,128]{2,1,0:T(8,128)}), f32[8,32,128]{2,1,0:T(8,128)S(1)}, u32[]{:S(2)}, u32[]{:S(2)}) async-start(f32[8,32,128]{2,1,0:T(8,128)} %broadcast_select_fusion), calls=%async_computation | async-start | bytes 262144 | tf_op jit(solution)/shard_map/all_to_all | solution.py:258
  15.9 0.0 copy-done.1
  15.9 0.1 reshape_squeeze.3
  15.9 7.3 %all-to-all-done = f32[8,32,128]{2,1,0:T(8,128)S(1)} async-done(((f32[8,32,128]{2,1,0:T(8,128)}), f32[8,32,128]{2,1,0:T(8,128)S(1)}, u32[]{:S(2)}, u32[]{:S(2)}) %all-to-all-start) | async-done | bytes 131104 | tf_op jit(solution)/shard_map/all_to_all | solution.py:258
  23.2 1.7 scatter_custom_fusion
  24.9 0.0 copy-start
  24.9 2.2 %copy-done = f32[8,512,256]{2,1,0:T(8,128)S(1)} copy-done((f32[8,512,256]{2,1,0:T(8,128)S(1)}, f32[8,512,256]{2,1,0:T(8,128)}, u32[]{:S(2)}) %copy-start) | copy-done | bytes 4194328
  27.1 149.9 %shard_map.82 = f32[8,64,128]{2,1,0:T(8,128)S(1)} custom-call(f32[8,2,2,64,128]{4,3,2,1,0:T(8,128)S(1)} %bitcast.24, f32[28,256,512]{2,1,0:T(8,128)} %lower_hbm.1, f32[8,512,256]{2,1,0:T(8,128)S(1)} %copy-done), custom_call_target="tpu_custom_call" | custom-call | tf_op jit(solution)/shard_map/pallas_call | solution.py:213
  177.0 0.7 copy.12
  (3 shorter events, 0.0 us)
Async XLA Ops:
  2.9 13.0 %copy-start.1 = (s32[1,1,8,32]{3,2,1,0:T(8,128)S(1)}, s32[1,1,8,32]{3,2,1,0:T(8,128)}, u32[]{:S(2)}) copy-start(s32[1,1,8,32]{3,2,1,0:T(8,128)} %param.13) | copy-start | bytes 3076
  8.5 14.7 %all-to-all-start = ((f32[8,32,128]{2,1,0:T(8,128)}), f32[8,32,128]{2,1,0:T(8,128)S(1)}, u32[]{:S(2)}, u32[]{:S(2)}) async-start(f32[8,32,128]{2,1,0:T(8,128)} %broadcast_select_fusion), calls=%async_computation | async-start | bytes 262144 | tf_op jit(solution)/shard_map/all_to_all | solution.py:258
  24.9 2.2 %copy-start = (f32[8,512,256]{2,1,0:T(8,128)S(1)}, f32[8,512,256]{2,1,0:T(8,128)}, u32[]{:S(2)}) copy-start(f32[8,512,256]{2,1,0:T(8,128)} %diag_hbm.1) | copy-start | bytes 12582916

commit v3 on v2

--- a/solution.py
+++ b/solution.py
@@ -10,13 +10,7 @@
 MESH = pl.DeviceIdType.MESH
 QUAD = 4
 CORES = 2
-
-
-def sweep_subdomain(field, radial_nu, tangent_nu, stride_value):
-    cell_index = jnp.arange(field.shape[0], dtype=jnp.int32)[:, None]
-    radial_prev = jnp.where(cell_index >= stride_value, jnp.roll(field, stride_value, axis=0), 0.0)
-    tangent_prev = jnp.where(cell_index >= 1, jnp.roll(field, 1, axis=0), 0.0)
-    return radial_nu * (field - radial_prev) + tangent_nu * (field - tangent_prev)
+PICKS = 8
 
 
 def pair_index(later_block, earlier_block):
@@ -36,9 +30,9 @@
 
 
 def solve_kernel(
-    n_row, n_col, rhs_ref, lower_hbm, diag_hbm, out_ref,
-    lower, diag, acc, c1_in, c2_src, c2_in, res, part, a_in, b_src, b_in, ysh, yb,
-    w_sem, d_sem, c1_sems, c2_sems, c3_sems, a_sems, b_sems, g_sems,
+    n_row, n_col, stride, counts, source, target_ref, field_hbm, nu_hbm, lower_hbm, diag_hbm,
+    out_ref, field, nu, picked, received, arrived, lower, diag, acc, c1_in, c2_src, c2_in, res, part, a_in, b_src, b_in, ysh, yb,
+    f_sem, p_sems, w_sem, d_sem, c1_sems, c2_sems, c3_sems, a_sems, b_sems, g_sems,
 ):
     blocks = diag.shape[0]
     n_quads = n_row // QUAD
@@ -56,7 +50,9 @@
     a_off = [lax.rem(a + s, QUAD) for s in range(1, QUAD)]
     a_peer = [{"row": b * QUAD + o} for o in a_off]
     b_peer = [{"row": lax.rem(b + s, n_quads) * QUAD + a} for s in range(1, n_quads)]
-    peers = [core_peer] + x_peer + a_peer + b_peer
+    row_at = [lax.rem(r + s, n_row) for s in range(n_row)]
+    peers = [core_peer] + x_peer + [{"row": g} for g in row_at[1:]]
+    slots = source.shape[2]
 
     def load_lower(k):
         return pltpu.make_async_copy(lower_hbm.at[k], lower.at[k], w_sem.at[k])
@@ -64,16 +60,17 @@
     def load_diag(k):
         return pltpu.make_async_copy(diag_hbm.at[k], diag.at[k], d_sem.at[k])
 
-    for i in range(blocks):
-        load_diag(i).start()
-        for j in range(i):
-            load_lower(pair_index(i, j)).start()
-
+    def load_cells():
+        return (
+            pltpu.make_async_copy(field_hbm, field, f_sem.at[0]),
+            pltpu.make_async_copy(nu_hbm, nu, f_sem.at[1]),
+        )
+
+    for copy in load_cells():
+        copy.start()
     barrier = pltpu.get_barrier_semaphore()
     for p in peers:
         pl.semaphore_signal(barrier, inc=1, device_id=p, device_id_type=MESH)
-    acc[...] = rhs_ref[...]
-    pl.semaphore_wait(barrier, len(peers))
 
     def remote(src, dst, sems, at, device):
         copy = pltpu.make_async_remote_copy(
@@ -87,6 +84,56 @@
         for copy in copies:
             copy.wait()
 
+    band = stride[0]
+
+    def pick(s):
+        g = row_at[s]
+        live_slots = counts[0, g]
+
+        def group(k8, carry):
+            for u in range(PICKS):
+                k = k8 * PICKS + u
+                m = source[0, g, k]
+                here = field[pl.ds(m, 1), :]
+                radial = field[pl.ds(jnp.maximum(m - band, 0), 1), :]
+                tangent = field[pl.ds(jnp.maximum(m - 1, 0), 1), :]
+                has_radial = jnp.where(m >= band, 1.0, 0.0)
+                has_tangent = jnp.where(m >= 1, 1.0, 0.0)
+                live = jnp.where(k < live_slots, 1.0, 0.0)
+                swept = nu[0, pl.ds(m, 1), :] * (here - radial * has_radial) + nu[
+                    1, pl.ds(m, 1), :
+                ] * (here - tangent * has_tangent)
+                picked[s, pl.ds(k, 1), :] = swept * live
+            return carry
+
+        lax.fori_loop(0, slots // PICKS, group, 0)
+
+    for copy in load_cells():
+        copy.wait()
+    for i in range(blocks):
+        load_diag(i).start()
+        for j in range(i):
+            load_lower(pair_index(i, j)).start()
+    sent = []
+    for s in range(1, n_row):
+        pick(s)
+        if s == 1:
+            pl.semaphore_wait(barrier, len(peers))
+        sent.append(remote(picked.at[s], received.at[r], p_sems, (s - 1,), {"row": row_at[s]}))
+    pick(0)
+    received[r] = picked[0]
+    finish(sent)
+    arrived[...] = halves(received[...].reshape(arrived.shape[0], rotor), 1)
+
+    def place(i):
+        rows = CORES * half_rows
+        here = lax.broadcasted_iota(jnp.int32, (rows, arrived.shape[0]), 0) + i * rows
+        chosen = jnp.where(here == target_ref[...], 1.0, 0.0).astype(jnp.bfloat16)
+        full = jnp.dot(chosen, arrived[...], preferred_element_type=jnp.float32)
+        acc[i] = (full[:, :rotor] + full[:, rotor:]).reshape(acc.shape[1:])
+
+    place(0)
+
     def lower_step(i, j):
         k = pair_index(i, j)
         load_lower(k).wait()
@@ -101,11 +148,17 @@
     def step(i, carry):
         parity = lax.rem(i, 2)
 
-        def deferred(*slots):
-            for t in slots:
+        def deferred(*turns):
+            for t in turns:
                 @pl.when(jnp.logical_and(i > 0, i + 1 + t < blocks))
                 def _():
                     lower_step(i + 1 + t, i - 1)
+
+            @pl.when(i == 0)
+            def _():
+                for t in turns:
+                    if 1 + t < blocks:
+                        place(1 + t)
 
         @pl.when(i > 0)
         def _():
@@ -180,7 +233,7 @@
                     remote(ysh.at[h, a], ysh.at[h, a], g_sems, (h, s), p)
                     for s, p in enumerate(a_peer)
                 ])
-            deferred(4, 5)
+            deferred(*range(4, blocks - 1))
             for h in range(n_quads):
                 finish(back[h])
             yb[...] = halves(ysh[...].reshape(yb.shape[0], rotor), 1)
@@ -196,9 +249,12 @@
     lax.fori_loop(0, blocks, step, 0)
 
 
-def solve(interface, lower_tiles, diag_inverse):
+def per_device(
+    sub_field, reluctivity, stride, counts, source_cell, target_row, lower_tiles, diag_inverse
+):
     n_row, n_col = lax.axis_size("row"), lax.axis_size("col")
-    blocks, tile_rows, rotor = interface.shape
+    blocks, tile_rows, rotor = diag_inverse.shape[0], lower_tiles.shape[1], sub_field.shape[1]
+    cap = source_cell.shape[2]
     pairs = lower_tiles.shape[0]
     share = diag_inverse.shape[1]
     piece = share // n_row
@@ -208,14 +264,20 @@
     col_chunk = (chunks, tile_rows // CORES // chunks, rotor)
     f32 = jnp.float32
     vmem = pl.BlockSpec(memory_space=pltpu.VMEM)
+    smem = pl.BlockSpec(memory_space=pltpu.SMEM)
     hbm = pl.BlockSpec(memory_space=pl.ANY)
     dma = pltpu.SemaphoreType.DMA
-    return pl.pallas_call(
+    pieces = pl.pallas_call(
         functools.partial(solve_kernel, n_row, n_col),
         out_shape=jax.ShapeDtypeStruct((blocks, piece, rotor), f32),
-        in_specs=[vmem, hbm, hbm],
+        in_specs=[smem, smem, smem, vmem, hbm, hbm, hbm, hbm],
         out_specs=vmem,
         scratch_shapes=[
+            pltpu.VMEM(sub_field.shape, f32),
+            pltpu.VMEM(reluctivity.shape, f32),
+            pltpu.VMEM((n_row, cap, rotor), f32),
+            pltpu.VMEM((n_row, cap, rotor), f32),
+            pltpu.VMEM((n_row * cap, 2 * rotor), jnp.bfloat16),
             pltpu.VMEM(lower_tiles.shape, f32),
             pltpu.VMEM(diag_inverse.shape, f32),
             pltpu.VMEM((blocks, CORES) + col_chunk, f32),
@@ -229,6 +291,8 @@
             pltpu.VMEM((2, quads, quads - 1, piece, rotor), f32),
             pltpu.VMEM((quads, QUAD, piece, rotor), f32),
             pltpu.VMEM((share, 2 * rotor), jnp.bfloat16),
+            dma((2,)),
+            dma((2, n_row - 1)),
             dma((pairs,)),
             dma((blocks,)),
             dma((2, chunks)),
@@ -241,29 +305,11 @@
         compiler_params=pltpu.CompilerParams(
             collective_id=0, has_side_effects=True, vmem_limit_bytes=48 * 1024 * 1024
         ),
-    )(interface.reshape((blocks, CORES) + col_chunk), lower_tiles, diag_inverse)
-
-
-def per_device(
-    sub_field, reluctivity, stride, counts, source_cell, target_row, lower_tiles, diag_inverse
-):
-    blocks = diag_inverse.shape[0]
-    tile_rows = lower_tiles.shape[1]
-    rotor = sub_field.shape[1]
-    swept = sweep_subdomain(sub_field, reluctivity[0], reluctivity[1], stride[0])
-    picked = swept[source_cell[0]]
-    slots = source_cell.shape[2]
-    live = jnp.arange(slots, dtype=jnp.int32)[None, :] < counts[0][:, None]
-    picked = jnp.where(live[:, :, None], picked, 0.0)
-    received = lax.all_to_all(picked, "row", split_axis=0, concat_axis=0, tiled=True)
-    targets = target_row[0, 0].reshape(-1)
-    interface = (
-        jnp.zeros((blocks * tile_rows, rotor), jnp.float32)
-        .at[targets]
-        .add(received.reshape(-1, rotor))
+    )(
+        stride, counts, source_cell, target_row.reshape(1, n_row * cap),
+        sub_field, reluctivity, lower_tiles, diag_inverse,
     )
-    interface = interface.reshape(blocks, tile_rows, rotor)
-    return solve(interface, lower_tiles, diag_inverse)[:, None]
+    return pieces[:, None]
 
 
 def solution(mesh):

time: 178 us -> 166 us (0.933)
  Pallas kernels: 150 us -> 160 us
  other arithmetic: 8.04 us -> 0 us
  starting transfers between devices: 7.31 us -> 0 us
  waiting for transfers between devices: 7.25 us -> 0 us
    pallas_call x1, Pallas kernels: 150 us -> 160 us  [per_device(): pl.pallas_call(functools.partial(solve_kernel, n_row, n_col), out_shape=j...]
    all_to_all x1 -> x0, starting transfers between devices: 7.31 us -> none  [per_device(): lax.all_to_all(picked, 'row', split_axis=0, concat_axis=0, tiled=True)]
    all_to_all x1 -> x0, waiting for transfers between devices: 7.25 us -> none  [per_device(): lax.all_to_all(picked, 'row', split_axis=0, concat_axis=0, tiled=True)]
    add x1 -> x0, other arithmetic: 4.17 us -> none  [sweep_subdomain(): radial_nu * (field - radial_prev) + tangent_nu * (field - tangent_prev)]
    unnamed x5 -> x9, local copies, waits for them, and re-layouts: 2.89 us -> 4.86 us
  transfers between devices with their start and end apart: 1 -> 0, of which waited for: 1 -> 0; matrix products, arithmetic and copies ran while one was open for 0% -> 0% of each run, Pallas kernels for 0% -> 0%
where the time goes in v3:
time: 166 us
  Pallas kernels  160 us (96%)
  local copies, waits for them, and re-layouts  5.63 us (3%)
    pallas_call x1, Pallas kernels, per_device(): pl.pallas_call(functools.partial(solve_kernel, n_row, n_col), out_shape=j...  160 us
    unnamed x9, local copies, waits for them, and re-layouts  4.86 us

profile of v3, /device:TPU:0, one launch (start us, length us, event | category | flops | bytes accessed | tf_op | source)
XLA Modules:
  0.0 166.2 jit_solution(12353423678061833176)
XLA Ops:
  0.7 0.8 reshape.3.target_ref
  1.4 0.0 copy-start
  1.4 1.6 copy-done
  3.0 0.0 copy-start.1
  3.0 1.2 copy-done.1
  4.2 0.0 copy-start.2
  4.2 0.7 copy-done.2
  4.9 0.0 copy-start.3
  4.9 0.7 copy-done.3
  5.6 159.9 %shard_map.82 = f32[8,64,128]{2,1,0:T(8,128)S(1)} custom-call(s32[1]{0:T(128)S(6)} %copy.11.stride, s32[1,8]{1,0:T(1,128)S(1)} %copy-done.3, s32[1,8,32]{2,1,0:T(8,128)S(1)} %copy-done.2, s32[1,256]{1,0:T(1,128)S(1)} %reshape.3.target_ref, f32[2048,128]{1,0:T(8,128)S(1)} %copy-done.1, f32[2,2048,128]{2,1,0:T(8,128)S(1)} %copy-done, ...), custom_call_target="tpu_custom_call" | custom-call | tf_op jit(solution)/shard_map/pallas_call | solution.py:270
  165.5 0.7 copy.12
Async XLA Ops:
  1.4 1.6 copy-start
  3.0 1.2 copy-start.1
  4.2 0.7 copy-start.2
  4.9 0.7 copy-start.3

commit v4 on v3

--- a/solution.py
+++ b/solution.py
@@ -11,6 +11,7 @@
 QUAD = 4
 CORES = 2
 PICKS = 8
+SPLIT = 2
 
 
 def pair_index(later_block, earlier_block):
@@ -53,6 +54,7 @@
     row_at = [lax.rem(r + s, n_row) for s in range(n_row)]
     peers = [core_peer] + x_peer + [{"row": g} for g in row_at[1:]]
     slots = source.shape[2]
+    strips = [(h, u) for h in range(n_quads) for u in range(SPLIT)]
 
     def load_lower(k):
         return pltpu.make_async_copy(lower_hbm.at[k], lower.at[k], w_sem.at[k])
@@ -199,51 +201,55 @@
         for h in range(n_quads):
             rows = diag[i, h * chunk_share:(h + 1) * chunk_share]
             part[h] = split_product(rows, residual).reshape(part.shape[1:])
-            a_copies.append([
-                remote(part.at[h, o], a_in.at[h, s], a_sems, (h, s), p)
-                for s, (o, p) in enumerate(zip(a_off, a_peer))
-            ])
+            a_copies += [
+                [
+                    remote(part.at[h, o, u], a_in.at[h, u, s], a_sems, (h, u, s), p)
+                    for s, (o, p) in enumerate(zip(a_off, a_peer))
+                ]
+                for u in range(SPLIT)
+            ]
         deferred(1, 2)
         b_copies = []
-        for h in range(n_quads):
-            finish(a_copies[h])
-            total = part[h, a]
+        for n, (h, u) in enumerate(strips):
+            finish(a_copies[n])
+            total = part[h, a, u]
             for s in range(QUAD - 1):
-                total = total + a_in[h, s]
-            b_src[h] = total
+                total = total + a_in[h, u, s]
+            b_src[n] = total
             b_copies.append([
-                remote(b_src.at[h], b_in.at[parity, h, s], b_sems, (parity, h, s), p)
+                remote(b_src.at[n], b_in.at[parity, n, s], b_sems, (parity, n, s), p)
                 for s, p in enumerate(b_peer)
             ])
         deferred(3)
 
-        def across(h):
-            finish(b_copies[h])
-            total = b_src[h]
+        def across(n):
+            h, u = strips[n]
+            finish(b_copies[n])
+            total = b_src[n]
             for s in range(n_quads - 1):
-                total = total + b_in[parity, h, s]
-            ysh[h, a] = total
+                total = total + b_in[parity, n, s]
+            ysh[h, a, u] = total
 
         @pl.when(i < blocks - 1)
         def _():
             back = []
-            for h in range(n_quads):
-                across(h)
+            for n, (h, u) in enumerate(strips):
+                across(n)
                 back.append([
-                    remote(ysh.at[h, a], ysh.at[h, a], g_sems, (h, s), p)
+                    remote(ysh.at[h, a, u], ysh.at[h, a, u], g_sems, (h, u, s), p)
                     for s, p in enumerate(a_peer)
                 ])
             deferred(*range(4, blocks - 1))
-            for h in range(n_quads):
-                finish(back[h])
+            for copies in back:
+                finish(copies)
             yb[...] = halves(ysh[...].reshape(yb.shape[0], rotor), 1)
 
         @pl.when(i == blocks - 1)
         def _():
-            for h in range(n_quads):
-                across(h)
-
-        out_ref[i] = ysh[b, a]
+            for n in range(len(strips)):
+                across(n)
+
+        out_ref[i] = ysh[b, a].reshape(out_ref.shape[1:])
         return carry
 
     lax.fori_loop(0, blocks, step, 0)
@@ -260,8 +266,9 @@
     piece = share // n_row
     quads = n_row // QUAD
     n_x = n_col // CORES
-    chunks = 2
+    chunks = 4
     col_chunk = (chunks, tile_rows // CORES // chunks, rotor)
+    strip = (piece // SPLIT, rotor)
     f32 = jnp.float32
     vmem = pl.BlockSpec(memory_space=pltpu.VMEM)
     smem = pl.BlockSpec(memory_space=pltpu.SMEM)
@@ -285,11 +292,11 @@
             pltpu.VMEM(col_chunk, f32),
             pltpu.VMEM((2, chunks, n_x - 1) + col_chunk[1:], f32),
             pltpu.VMEM((CORES,) + col_chunk, f32),
-            pltpu.VMEM((quads, QUAD, piece, rotor), f32),
-            pltpu.VMEM((quads, QUAD - 1, piece, rotor), f32),
-            pltpu.VMEM((quads, piece, rotor), f32),
-            pltpu.VMEM((2, quads, quads - 1, piece, rotor), f32),
-            pltpu.VMEM((quads, QUAD, piece, rotor), f32),
+            pltpu.VMEM((quads, QUAD, SPLIT) + strip, f32),
+            pltpu.VMEM((quads, SPLIT, QUAD - 1) + strip, f32),
+            pltpu.VMEM((quads * SPLIT,) + strip, f32),
+            pltpu.VMEM((2, quads * SPLIT, quads - 1) + strip, f32),
+            pltpu.VMEM((quads, QUAD, SPLIT) + strip, f32),
             pltpu.VMEM((share, 2 * rotor), jnp.bfloat16),
             dma((2,)),
             dma((2, n_row - 1)),
@@ -298,9 +305,9 @@
             dma((2, chunks)),
             dma((2, 2, chunks, n_x - 1)),
             dma((2, chunks)),
-            dma((2, quads, QUAD - 1)),
-            dma((2, 2, quads, quads - 1)),
-            dma((2, quads, QUAD - 1)),
+            dma((2, quads, SPLIT, QUAD - 1)),
+            dma((2, 2, quads * SPLIT, quads - 1)),
+            dma((2, quads, SPLIT, QUAD - 1)),
         ],
         compiler_params=pltpu.CompilerParams(
             collective_id=0, has_side_effects=True, vmem_limit_bytes=48 * 1024 * 1024

time: 166 us -> 162 us (0.976)
  Pallas kernels: 160 us -> 155 us
    pallas_call x1, Pallas kernels: 160 us -> 155 us  [per_device(): pl.pallas_call(functools.partial(solve_kernel, n_row, n_col), out_shape=j...]
where the time goes in v4:
time: 162 us; the launch traced here: 161 us
  Pallas kernels  155 us (96%)
  local copies, waits for them, and re-layouts  5.63 us (3%)
    pallas_call x1, Pallas kernels, per_device(): pl.pallas_call(functools.partial(solve_kernel, n_row, n_col), out_shape=j...  155 us
    unnamed x9, local copies, waits for them, and re-layouts  4.86 us

profile of v4, /device:TPU:0, one launch (start us, length us, event | category | flops | bytes accessed | tf_op | source)
XLA Modules:
  0.0 161.3 jit_solution(5334532931107164950)
XLA Ops:
  0.7 0.8 reshape.3.target_ref
  1.4 0.0 copy-start
  1.4 1.6 copy-done
  3.0 0.0 copy-start.1
  3.0 1.2 copy-done.1
  4.2 0.0 copy-start.2
  4.2 0.7 copy-done.2
  4.9 0.0 copy-start.3
  4.9 0.7 copy-done.3
  5.6 155.0 %shard_map.82 = f32[8,64,128]{2,1,0:T(8,128)S(1)} custom-call(s32[1]{0:T(128)S(6)} %copy.11.stride, s32[1,8]{1,0:T(1,128)S(1)} %copy-done.3, s32[1,8,32]{2,1,0:T(8,128)S(1)} %copy-done.2, s32[1,256]{1,0:T(1,128)S(1)} %reshape.3.target_ref, f32[2048,128]{1,0:T(8,128)S(1)} %copy-done.1, f32[2,2048,128]{2,1,0:T(8,128)S(1)} %copy-done, ...), custom_call_target="tpu_custom_call" | custom-call | tf_op jit(solution)/shard_map/pallas_call | solution.py:277
  160.6 0.7 copy.12
Async XLA Ops:
  1.4 1.6 copy-start
  3.0 1.2 copy-start.1
  4.2 0.7 copy-start.2
  4.9 0.7 copy-start.3

commit v5 on v4

--- a/solution.py
+++ b/solution.py
@@ -31,8 +31,8 @@
 
 
 def solve_kernel(
-    n_row, n_col, stride, counts, source, target_ref, field_hbm, nu_hbm, lower_hbm, diag_hbm,
-    out_ref, field, nu, picked, received, arrived, lower, diag, acc, c1_in, c2_src, c2_in, res, part, a_in, b_src, b_in, ysh, yb,
+    n_row, n_col, stride, counts_hbm, source_hbm, target_hbm, field_hbm, nu_hbm, lower_hbm,
+    diag_hbm, out_ref, counts, source, target_rows, field, nu, picked, received, arrived, lower, diag, acc, c1_in, c2_src, c2_in, res, part, a_in, b_src, b_in, ysh, yb,
     f_sem, p_sems, w_sem, d_sem, c1_sems, c2_sems, c3_sems, a_sems, b_sems, g_sems,
 ):
     blocks = diag.shape[0]
@@ -64,6 +64,9 @@
 
     def load_cells():
         return (
+            pltpu.make_async_copy(counts_hbm, counts, f_sem.at[3]),
+            pltpu.make_async_copy(source_hbm, source, f_sem.at[4]),
+            pltpu.make_async_copy(target_hbm.at[0, 0], target_rows, f_sem.at[2]),
             pltpu.make_async_copy(field_hbm, field, f_sem.at[0]),
             pltpu.make_async_copy(nu_hbm, nu, f_sem.at[1]),
         )
@@ -86,10 +89,9 @@
         for copy in copies:
             copy.wait()
 
-    band = stride[0]
-
     def pick(s):
         g = row_at[s]
+        band = stride[0]
         live_slots = counts[0, g]
 
         def group(k8, carry):
@@ -127,10 +129,12 @@
     finish(sent)
     arrived[...] = halves(received[...].reshape(arrived.shape[0], rotor), 1)
 
+    targets = jnp.concatenate([target_rows[q:q + 1, :] for q in range(n_row)], axis=1)
+
     def place(i):
         rows = CORES * half_rows
         here = lax.broadcasted_iota(jnp.int32, (rows, arrived.shape[0]), 0) + i * rows
-        chosen = jnp.where(here == target_ref[...], 1.0, 0.0).astype(jnp.bfloat16)
+        chosen = jnp.where(here == targets, 1.0, 0.0).astype(jnp.bfloat16)
         full = jnp.dot(chosen, arrived[...], preferred_element_type=jnp.float32)
         acc[i] = (full[:, :rotor] + full[:, rotor:]).reshape(acc.shape[1:])
 
@@ -271,15 +275,17 @@
     strip = (piece // SPLIT, rotor)
     f32 = jnp.float32
     vmem = pl.BlockSpec(memory_space=pltpu.VMEM)
-    smem = pl.BlockSpec(memory_space=pltpu.SMEM)
-    hbm = pl.BlockSpec(memory_space=pl.ANY)
+    hbm = pl.BlockSpec(memory_space=pltpu.HBM)
     dma = pltpu.SemaphoreType.DMA
     pieces = pl.pallas_call(
         functools.partial(solve_kernel, n_row, n_col),
         out_shape=jax.ShapeDtypeStruct((blocks, piece, rotor), f32),
-        in_specs=[smem, smem, smem, vmem, hbm, hbm, hbm, hbm],
+        in_specs=[pl.BlockSpec(memory_space=pltpu.SMEM)] + [hbm] * 7,
         out_specs=vmem,
         scratch_shapes=[
+            pltpu.SMEM(counts.shape, jnp.int32),
+            pltpu.SMEM(source_cell.shape, jnp.int32),
+            pltpu.VMEM((n_row, cap), jnp.int32),
             pltpu.VMEM(sub_field.shape, f32),
             pltpu.VMEM(reluctivity.shape, f32),
             pltpu.VMEM((n_row, cap, rotor), f32),
@@ -298,7 +304,7 @@
             pltpu.VMEM((2, quads * SPLIT, quads - 1) + strip, f32),
             pltpu.VMEM((quads, QUAD, SPLIT) + strip, f32),
             pltpu.VMEM((share, 2 * rotor), jnp.bfloat16),
-            dma((2,)),
+            dma((5,)),
             dma((2, n_row - 1)),
             dma((pairs,)),
             dma((blocks,)),
@@ -310,11 +316,10 @@
             dma((2, quads, SPLIT, QUAD - 1)),
         ],
         compiler_params=pltpu.CompilerParams(
-            collective_id=0, has_side_effects=True, vmem_limit_bytes=48 * 1024 * 1024
+            collective_id=0, has_side_effects=True, vmem_limit_bytes=67043328
         ),
     )(
-        stride, counts, source_cell, target_row.reshape(1, n_row * cap),
-        sub_field, reluctivity, lower_tiles, diag_inverse,
+        stride, counts, source_cell, target_row, sub_field, reluctivity, lower_tiles, diag_inverse
     )
     return pieces[:, None]
 

time: 162 us -> 157 us (0.969)
  local copies, waits for them, and re-layouts: 5.63 us -> 1.67 us
    unnamed x9 -> x1, local copies, waits for them, and re-layouts: 4.86 us -> 1.67 us
where the time goes in v5:
time: 157 us
  Pallas kernels  155 us (99%)
  local copies, waits for them, and re-layouts  1.67 us (1%)
    pallas_call x1, Pallas kernels, per_device(): pl.pallas_call(functools.partial(solve_kernel, n_row, n_col), out_shape=j...  155 us

profile of v5, /device:TPU:0, one launch (start us, length us, event | category | flops | bytes accessed | tf_op | source)
XLA Modules:
  0.0 157.2 jit_solution(6316659891346345185)
XLA Ops:
  0.7 154.9 %shard_map.82 = f32[8,64,128]{2,1,0:T(8,128)} custom-call(s32[1]{0:T(128)S(6)} %copy.11.stride, s32[1,8]{1,0:T(1,128)} %counts_hbm.1, s32[1,8,32]{2,1,0:T(8,128)} %source_hbm.1, s32[1,1,8,32]{3,2,1,0:T(8,128)} %target_hbm.1, f32[2048,128]{1,0:T(8,128)} %field_hbm.1, f32[2,2048,128]{2,1,0:T(8,128)} %nu_hbm.1, f32[28,256,512]{2,1,0:T(8,128)} %lower_hbm.1, ...), custom_call_target="tpu_custom_call" | custom-call | tf_op jit(solution)/shard_map/pallas_call | solution.py:280
  155.6 1.7 %copy.12 = f32[8,1,64,128]{3,2,1,0:T(8,128)} copy(f32[8,1,64,128]{3,2,1,0:T(8,128)} %bitcast.3) | data formatting | bytes 524288
